TPU v7x, 128 devices: a whole 4x4x4 slice. The times are simulated.
128 devices in a mesh: stream: 8 (over x, z_lo), span: 16 (over y, z_hi, core).
Axes of the slice: x: 4, y: 4, z: 4 (z_hi: 2, z_lo: 2; z = z_hi * 2 + z_lo), core: 2. Of those that a mesh axis runs over, the one named last changes fastest.
Arguments:
- right_side: float32 [4, 262144], P(None, ('stream', 'span')), may hold values from -5 to 6
- fine_values: float32 [8, 4, 4, 262144], P(None, None, None, ('stream', 'span')), as said below
- fine_columns: int32 [8, 262144], P(None, ('stream', 'span')), may hold values from 0 to 2303, as said below
- fine_sends: int32 [4, 8192], P(None, ('stream', 'span')), may hold values from 0 to 2047, as said below
- fine_order: int32 [128, 2048], P(('stream', 'span')), may hold values from 0 to 2047, each once within a row
- fine_weights: float32 [4, 4, 262144], P(None, None, ('stream', 'span')), may hold values from -0.6 to 1.2
- middle_values: float32 [8, 4, 4, 65536], P(None, None, None, ('stream', 'span')), as said below
- middle_columns: int32 [8, 65536], P(None, ('stream', 'span')), may hold values from 0 to 767, as said below
- middle_sends: int32 [4, 8192], P(None, ('stream', 'span')), may hold values from 0 to 511, as said below
- middle_order: int32 [128, 512], P(('stream', 'span')), may hold values from 0 to 511, each once within a row
- middle_weights: float32 [4, 4, 65536], P(None, None, ('stream', 'span')), may hold values from -0.6 to 1.2
- coarsest_values: float32 [8, 4, 4, 16384], P(None, None, None, ('stream', 'span')), as said below
- coarsest_columns: int32 [8, 16384], P(None, ('stream', 'span')), may hold values from 0 to 2047, as said below
Outputs:
- solution: float32 [4, 262144], P(None, ('stream', 'span'))
- residual: float32 [4, 262144], P(None, ('stream', 'span'))
Inputs may be any that keep to these rules, and one draw needn't show every extreme that they name: `fine_sends`: entry [d, p * 64 + s] is a local row block of device p sent in direction d (0: lower stream index, 1: higher stream index, 2: lower span index, 3: higher span index). Each list has a length of at most 64, which differs between devices and directions and is 64 on some device; rows may repeat within a list, and the slots at or after the length repeat the list's slot 0 as padding. `middle_sends`: as for the first level, with local row blocks of the second level. `fine_columns`: block k = 0 of row block n names its own local row. Entries below 2048 are local row blocks; an entry 2048 + e * 64 + s names slot s of halo block e. Where halo block e has a sending device, s is below the length of that device's list; where it has none (the block is zero), s may be any slot below 64. `middle_columns`: as for the first level with 512 local row blocks. `coarsest_columns`: block k = 0 names the row block itself within its slab; the others name row blocks of the same slab. `fine_values`: each diagonal entry of the k = 0 block is 1 or more, and the other 31 entries of its row over all 8 blocks have absolute values summing to at most 0.9 times it. `middle_values`: as for the first level. `coarsest_values`: as for the first level.
All inputs are finite; a program needn't handle non-finite values.
Results may differ from a plain program's by a relative error of at most 0.0003.
Values sent between devices are 32-bit elements; how exact they have to be, the bound alone decides.
A program may use at most 64 MiB of HBM per device.

v0:
```python
import math
import jax
import jax.numpy as jnp
from jax import lax
from jax.sharding import PartitionSpec as P

KSM = 3
KC = 4
CHEB_CENTRE = 1.0
CHEB_RADIUS = 0.9


def padded(cells, sides, width, closed):
    for axis, dim in sides:
        count = lax.axis_size(axis)
        ends = count if closed else count - 1
        head = lax.slice_in_dim(cells, 0, width, axis=dim)
        tail = lax.slice_in_dim(cells, cells.shape[dim] - width, cells.shape[dim], axis=dim)
        cells = jnp.concatenate(
            [
                lax.ppermute(tail, axis, [(i, (i + 1) % count) for i in range(ends)]),
                cells,
                lax.ppermute(head, axis, [((i + 1) % count, i) for i in range(ends)]),
            ],
            axis=dim,
        )
    return cells


def chebyshev(operate, inverse_diag, target, initial, degree):
    sigma_value = CHEB_CENTRE / CHEB_RADIUS
    rho_prev = 1.0 / sigma_value
    if initial is None:
        iterate = jnp.zeros_like(target)
        current = target
    else:
        iterate = initial
        current = target - operate(initial)
    update = inverse_diag * current / CHEB_CENTRE
    iterate = iterate + update
    for _ in range(degree - 1):
        rho_next = 1.0 / (2.0 * sigma_value - rho_prev)
        current = target - operate(iterate)
        update = rho_next * rho_prev * update + 2.0 * rho_next / CHEB_RADIUS * (
            inverse_diag * current
        )
        iterate = iterate + update
        rho_prev = rho_next
    return iterate


def inverse_diagonal(values):
    identity = jnp.eye(4, dtype=values.dtype)
    return 1.0 / jnp.sum(values[0] * identity[:, :, None], axis=1)


def split_parts(vector):
    high_part = vector.astype(jnp.bfloat16)
    rest_part = vector - lax.optimization_barrier(high_part).astype(jnp.float32)
    middle_part = rest_part.astype(jnp.bfloat16)
    low_part = (rest_part - lax.optimization_barrier(middle_part).astype(jnp.float32)).astype(
        jnp.bfloat16
    )
    return jnp.concatenate([high_part, middle_part, low_part], axis=0)


def join_parts(product, row_count):
    return product[:row_count] + product[row_count : 2 * row_count] + product[2 * row_count :]


def pick_columns(vector, index_flat):
    parts = split_parts(vector)
    width = parts.shape[1]
    total = index_flat.shape[0]
    block_size = math.gcd(total, 2048)
    places = jnp.arange(width, dtype=jnp.int32)[:, None]

    def one_block(index_block):
        select = (places == index_block[None, :]).astype(jnp.bfloat16)
        return jnp.dot(parts, select, preferred_element_type=jnp.float32)

    picked = lax.map(one_block, index_flat.reshape(total // block_size, block_size))
    picked = jnp.moveaxis(picked, 0, 1).reshape(parts.shape[0], total)
    return join_parts(picked, vector.shape[0])


def extend(vector, send_rows):
    halo_width = send_rows.shape[1]
    outgoing = pick_columns(vector, send_rows.reshape(-1)).reshape(4, 4, halo_width)
    stream_pair = jnp.concatenate([outgoing[:, 0], outgoing[:, 1]], axis=1)
    span_pair = jnp.concatenate([outgoing[:, 2], outgoing[:, 3]], axis=1)
    stream_ext = padded(stream_pair, (("stream", 1),), halo_width, True)
    span_ext = padded(span_pair, (("span", 1),), halo_width, False)
    return jnp.concatenate(
        [
            vector,
            stream_ext[:, :halo_width],
            stream_ext[:, 3 * halo_width :],
            span_ext[:, :halo_width],
            span_ext[:, 3 * halo_width :],
        ],
        axis=1,
    )


def block_product(values, gathered):
    return jnp.einsum("kijn,jkn->in", values, gathered, precision=lax.Precision.HIGHEST)


def apply_level(vector, values, columns, send_rows):
    extended_vec = extend(vector, send_rows)
    picked = pick_columns(extended_vec, columns.reshape(-1)).reshape(
        4, columns.shape[0], columns.shape[1]
    )
    return block_product(values, picked)


def membership(order_rows):
    row_count = order_rows.shape[0]
    grouped = order_rows.reshape(row_count // 4, 4)
    places = jnp.arange(row_count, dtype=jnp.int32)[:, None, None]
    return jnp.any(places == grouped[None, :, :], axis=2).astype(jnp.bfloat16)


def restrict(fine_vec, weights, member):
    product = jnp.einsum("ijn,in->jn", weights, fine_vec, precision=lax.Precision.HIGHEST)
    parts = split_parts(product)
    return join_parts(jnp.dot(parts, member, preferred_element_type=jnp.float32), 4)


def prolong(coarse, weights, member):
    parts = split_parts(coarse)
    spread = join_parts(
        lax.dot_general(
            parts, member, (((1,), (1,)), ((), ())), preferred_element_type=jnp.float32
        ),
        4,
    )
    return jnp.einsum("ijn,jn->in", weights, spread, precision=lax.Precision.HIGHEST)


def per_device(
    right_side,
    fine_values,
    fine_columns,
    fine_sends,
    fine_order,
    fine_weights,
    middle_values,
    middle_columns,
    middle_sends,
    middle_order,
    middle_weights,
    coarsest_values,
    coarsest_columns,
):

    def fine_apply(vector):
        return apply_level(vector, fine_values, fine_columns, fine_sends)

    def middle_apply(vector):
        return apply_level(vector, middle_values, middle_columns, middle_sends)

    fine_inv = inverse_diagonal(fine_values)
    middle_inv = inverse_diagonal(middle_values)
    fine_member = membership(fine_order[0])
    middle_member = membership(middle_order[0])
    first_iter = chebyshev(fine_apply, fine_inv, right_side, None, KSM)
    fine_resid = right_side - fine_apply(first_iter)
    middle_rhs = restrict(fine_resid, fine_weights, fine_member)
    middle_iter = chebyshev(middle_apply, middle_inv, middle_rhs, None, KSM)
    middle_resid = middle_rhs - middle_apply(middle_iter)
    coarse_rhs = restrict(middle_resid, middle_weights, middle_member)
    own_rows = coarse_rhs.shape[1]
    group_rhs, group_values = (
        lax.all_gather(coarse_rhs, "span", axis=1, tiled=True),
        lax.all_gather(coarsest_values, "span", axis=3, tiled=True),
    )
    group_columns = lax.all_gather(coarsest_columns, "span", axis=1, tiled=True)

    def group_apply(vector):
        return block_product(group_values, vector[:, group_columns])

    group_iter = chebyshev(group_apply, inverse_diagonal(group_values), group_rhs, None, KC)
    coarse_iter = lax.dynamic_slice_in_dim(
        group_iter, lax.axis_index("span") * own_rows, own_rows, 1
    )
    middle_start = middle_iter + prolong(coarse_iter, middle_weights, middle_member)
    middle_final = chebyshev(middle_apply, middle_inv, middle_rhs, middle_start, KSM)
    fine_start = first_iter + prolong(middle_final, fine_weights, fine_member)
    solution = chebyshev(fine_apply, fine_inv, right_side, fine_start, KSM)
    residual = right_side - fine_apply(solution)
    return (solution, residual)


def solution(mesh):
    in_specs = (
        P(None, ("stream", "span")),
        P(None, None, None, ("stream", "span")),
        P(None, ("stream", "span")),
        P(None, ("stream", "span")),
        P(("stream", "span"), None),
        P(None, None, ("stream", "span")),
        P(None, None, None, ("stream", "span")),
        P(None, ("stream", "span")),
        P(None, ("stream", "span")),
        P(("stream", "span"), None),
        P(None, None, ("stream", "span")),
        P(None, None, None, ("stream", "span")),
        P(None, ("stream", "span")),
    )
    out_specs = (P(None, ("stream", "span")), P(None, ("stream", "span")))
    return jax.shard_map(
        per_device, mesh=mesh, in_specs=in_specs, out_specs=out_specs, check_vma=False
    )
```

profile of v0, /device:TPU:1, one launch (start us, length us, event | category | flops | bytes accessed | tf_op | source)
XLA Modules:
  0.0 694.1 jit_solution(7039340005807783666)
XLA Ops:
  10.9 48.5 %all-gather.2.cloned.1.call-done = f32[8,4,4,2048]{3,2,1,0:T(4,128)} async-done(((f32[8,4,4,128]{3,2,1,0:T(4,128)}), f32[8,4,4,2048]{3,2,1,0:T(4,128)}) %all-gather.2.cloned.1.call-update) | async-done | bytes 1048592 | tf_op jit(solution)/shard_map/all_gather | solution.py:177
  71.2 6.1 fusion.78
  77.6 30.0 %while.39 = (s32[]{:T(128)}, f32[8,12,2048]{2,1,0:T(8,128)S(1)}, s32[8,2048]{1,0:T(8,128)}, bf16[12,2304]{1,0:T(8,128)(2,1)S(1)}, s32[]{:T(128)}) while((s32[]{:T(128)}, f32[8,12,2048]{2,1,0:T(8,128)S(1)}, s32[8,2048]{1,0:T(8,128)}, bf16[12,2304]{1,0:T(8,128)(2,1)S(1)}, s32[]{:T(128)}) %tuple.301), condition=%wide.region_2.0_spmd.clone, body=%wide.region_1.0_spmd.clone.sunk | while | flops 117964800 | bytes 229445 | solution.py:82
  112.6 5.7 collective-permute-start.6
  125.0 23.3 %while.40 = (s32[]{:T(128)}, f32[8,12,2048]{2,1,0:T(8,128)S(1)}, s32[8,2048]{1,0:T(8,128)S(1)}, bf16[12,2304]{1,0:T(8,128)(2,1)S(1)}, s32[]{:T(128)}) while((s32[]{:T(128)}, f32[8,12,2048]{2,1,0:T(8,128)S(1)}, s32[8,2048]{1,0:T(8,128)S(1)}, bf16[12,2304]{1,0:T(8,128)(2,1)S(1)}, s32[]{:T(128)}) %tuple.347), condition=%wide.region_4.5_spmd.clone, body=%wide.region_3.0_spmd.clone.sunk | while | flops 117964800 | bytes 229445 | solution.py:82
  157.7 26.1 %all_gather.11 = s32[8,2048]{1,0:T(8,128)} all-gather(s32[8,128]{1,0:T(8,128)S(1)} %copy-done.30), channel_id=1, replica_groups=mesh['stream'=8,'span'=16] {'span'}, dimensions={1}, use_global_device_ids=true | all-gather | bytes 69632 | tf_op jit(solution)/shard_map/all_gather | solution.py:179
  185.4 30.5 %while.41 = (s32[]{:T(128)}, f32[8,12,2048]{2,1,0:T(8,128)S(1)}, s32[8,2048]{1,0:T(8,128)S(1)}, bf16[12,2304]{1,0:T(8,128)(2,1)}, s32[]{:T(128)}) while((s32[]{:T(128)}, f32[8,12,2048]{2,1,0:T(8,128)S(1)}, s32[8,2048]{1,0:T(8,128)S(1)}, bf16[12,2304]{1,0:T(8,128)(2,1)}, s32[]{:T(128)}) %tuple.348), condition=%wide.region_7.8_spmd.clone, body=%wide.region_6.7_spmd.clone.sunk | while | flops 117964800 | bytes 211013 | solution.py:82
  222.0 5.4 collective-permute-start.14
  268.6 19.3 %all_gather.10 = f32[4,2048]{1,0:T(4,128)S(1)} all-gather(f32[4,128]{1,0:T(4,128)S(1)} %slice_add_fusion.58), channel_id=1, replica_groups=mesh['stream'=8,'span'=16] {'span'}, dimensions={1}, use_global_device_ids=true | all-gather | bytes 34816 | tf_op jit(solution)/shard_map/all_gather | solution.py:176
  289.0 54.8 %gather_fusion = f32[16384,4]{1,0:T(8,128)} fusion(f32[4,2048]{0,1:T(8,128)S(1)} %copy.181, s32[16384]{0:T(1024)S(1)} %broadcast_clamp_fusion), kind=kCustom, calls=%fused_computation | custom fusion | bytes 589824 | tf_op jit(solution)/shard_map/gather | solution.py:182
  343.8 5.3 copy.404
  351.8 60.0 %gather_fusion.1 = f32[16384,4]{1,0:T(8,128)} fusion(f32[4,2048]{0,1:T(8,128)S(1)} %copy.182, s32[16384]{0:T(1024)} %copy-done.5), kind=kCustom, calls=%fused_computation.1 | custom fusion | bytes 589824 | tf_op jit(solution)/shard_map/gather | solution.py:182
  411.8 5.2 copy.405
  419.2 60.0 %gather_fusion.2 = f32[16384,4]{1,0:T(8,128)} fusion(f32[4,2048]{0,1:T(8,128)S(1)} %copy.183, s32[16384]{0:T(1024)} %copy-done.5), kind=kCustom, calls=%fused_computation.2 | custom fusion | bytes 589824 | tf_op jit(solution)/shard_map/gather | solution.py:182
  479.3 5.3 copy.406
  510.2 4.4 collective-permute-done.31
  542.7 5.0 collective-permute-done.39
  548.0 23.3 %while.48 = (s32[]{:T(128)}, f32[8,12,2048]{2,1,0:T(8,128)S(1)}, s32[8,2048]{1,0:T(8,128)S(1)}, bf16[12,2304]{1,0:T(8,128)(2,1)S(1)}, s32[]{:T(128)}) while((s32[]{:T(128)}, f32[8,12,2048]{2,1,0:T(8,128)S(1)}, s32[8,2048]{1,0:T(8,128)S(1)}, bf16[12,2304]{1,0:T(8,128)(2,1)S(1)}, s32[]{:T(128)}) %tuple.349), condition=%wide.region_24.25_spmd.clone, body=%wide.region_23.24_spmd.clone.sunk | while | flops 117964800 | bytes 229445 | solution.py:82
  580.5 5.3 collective-permute-done.43
  586.1 23.3 %while.49 = (s32[]{:T(128)}, f32[8,12,2048]{2,1,0:T(8,128)S(1)}, s32[8,2048]{1,0:T(8,128)S(1)}, bf16[12,2304]{1,0:T(8,128)(2,1)S(1)}, s32[]{:T(128)}) while((s32[]{:T(128)}, f32[8,12,2048]{2,1,0:T(8,128)S(1)}, s32[8,2048]{1,0:T(8,128)S(1)}, bf16[12,2304]{1,0:T(8,128)(2,1)S(1)}, s32[]{:T(128)}) %tuple.350), condition=%wide.region_26.27_spmd.clone, body=%wide.region_25.26_spmd.clone.sunk | while | flops 117964800 | bytes 229445 | solution.py:82
  618.9 5.1 collective-permute-done.47
  624.3 23.3 %while.50 = (s32[]{:T(128)}, f32[8,12,2048]{2,1,0:T(8,128)S(1)}, s32[8,2048]{1,0:T(8,128)S(1)}, bf16[12,2304]{1,0:T(8,128)(2,1)S(1)}, s32[]{:T(128)}) while((s32[]{:T(128)}, f32[8,12,2048]{2,1,0:T(8,128)S(1)}, s32[8,2048]{1,0:T(8,128)S(1)}, bf16[12,2304]{1,0:T(8,128)(2,1)S(1)}, s32[]{:T(128)}) %tuple.351), condition=%wide.region_28.29_spmd.clone, body=%wide.region_27.28_spmd.clone.sunk | while | flops 117964800 | bytes 229445 | solution.py:82
  656.8 5.3 collective-permute-done.51
  662.5 23.3 %while.51 = (s32[]{:T(128)}, f32[8,12,2048]{2,1,0:T(8,128)S(1)}, s32[8,2048]{1,0:T(8,128)S(1)}, bf16[12,2304]{1,0:T(8,128)(2,1)S(1)}, s32[]{:T(128)}) while((s32[]{:T(128)}, f32[8,12,2048]{2,1,0:T(8,128)S(1)}, s32[8,2048]{1,0:T(8,128)S(1)}, bf16[12,2304]{1,0:T(8,128)(2,1)S(1)}, s32[]{:T(128)}) %tuple.352), condition=%wide.region_30.31_spmd.clone, body=%wide.region_29.30_spmd.clone.sunk | while | flops 117964800 | bytes 229445 | solution.py:82
  (582 shorter events, 362.8 us)
Async XLA Ops:
  7.2 52.2 %all-gather.2.cloned.1.call-start = ((), (), s32[]{:S(2)}) async-start(), calls=%async_computation | async-start | bytes 1114112 | tf_op jit(solution)/shard_map/all_gather | solution.py:177
  62.6 14.6 %collective-permute-start = (f32[4,64]{1,0:T(4,128)S(1)}, f32[4,64]{1,0:T(4,128)S(1)}, u32[]{:S(2)}, u32[]{:S(2)}) collective-permute-start(f32[4,64]{1,0:T(4,128)S(1)} %bitcast.712), channel_id=1, source_target_pairs={{0,16},{16,32},{32,48},{48,64},{64,80},{80,96},{96,112},{112,0},{1... | collective-permute-start | bytes 3080 | tf_op jit(solution)/shard_map/ppermute | solution.py:21
  63.1 14.2 %collective-permute-start.1 = (f32[4,64]{1,0:T(4,128)S(1)}, f32[4,64]{1,0:T(4,128)S(1)}, u32[]{:S(2)}, u32[]{:S(2)}) collective-permute-start(f32[4,64]{1,0:T(4,128)S(1)} %bitcast.701), channel_id=1, source_target_pairs={{16,0},{32,16},{48,32},{64,48},{80,64},{96,80},{112,96},{0,112},{1... | collective-permute-start | bytes 3080 | tf_op jit(solution)/shard_map/ppermute | solution.py:23
  66.3 11.0 %collective-permute-start.2 = (f32[4,64]{1,0:T(4,128)S(1)}, f32[4,64]{1,0:T(4,128)S(1)}, u32[]{:S(2)}, u32[]{:S(2)}) collective-permute-start(f32[4,64]{1,0:T(4,128)S(1)} %bitcast.689), channel_id=1, source_target_pairs={{0,1},{1,2},{2,3},{3,4},{4,5},{5,6},{6,7},{7,8},{8,9},{9,10},{10,1... | collective-permute-start | bytes 3080 | tf_op jit(solution)/shard_map/ppermute | solution.py:21
  108.8 11.6 %collective-permute-start.4 = (f32[4,64]{1,0:T(4,128)S(1)}, f32[4,64]{1,0:T(4,128)S(1)}, u32[]{:S(2)}, u32[]{:S(2)}) collective-permute-start(f32[4,64]{1,0:T(4,128)S(1)} %bitcast.713), channel_id=1, source_target_pairs={{0,16},{16,32},{32,48},{48,64},{64,80},{80,96},{96,112},{112,0},{1... | collective-permute-start | bytes 3080 | tf_op jit(solution)/shard_map/ppermute | solution.py:21
  108.8 11.5 %collective-permute-start.5 = (f32[4,64]{1,0:T(4,128)S(1)}, f32[4,64]{1,0:T(4,128)S(1)}, u32[]{:S(2)}, u32[]{:S(2)}) collective-permute-start(f32[4,64]{1,0:T(4,128)S(1)} %bitcast.702), channel_id=1, source_target_pairs={{16,0},{32,16},{48,32},{64,48},{80,64},{96,80},{112,96},{0,112},{1... | collective-permute-start | bytes 3080 | tf_op jit(solution)/shard_map/ppermute | solution.py:23
  149.5 34.9 %collective-permute-start.10 = (f32[4,64]{1,0:T(4,128)S(1)}, f32[4,64]{1,0:T(4,128)S(1)}, u32[]{:S(2)}, u32[]{:S(2)}) collective-permute-start(f32[4,64]{1,0:T(4,128)S(1)} %bitcast.714), channel_id=1, source_target_pairs={{0,1},{1,2},{2,3},{3,4},{4,5},{5,6},{6,7},{7,8},{8,9},{9,10},{10,1... | collective-permute-start | bytes 3080 | tf_op jit(solution)/shard_map/ppermute | solution.py:21
  152.1 32.3 %collective-permute-start.11 = (f32[4,64]{1,0:T(4,128)S(1)}, f32[4,64]{1,0:T(4,128)S(1)}, u32[]{:S(2)}, u32[]{:S(2)}) collective-permute-start(f32[4,64]{1,0:T(4,128)S(1)} %bitcast.703), channel_id=1, source_target_pairs={{1,0},{2,1},{3,2},{4,3},{5,4},{6,5},{7,6},{8,7},{9,8},{10,9},{11,1... | collective-permute-start | bytes 3080 | tf_op jit(solution)/shard_map/ppermute | solution.py:23
  154.0 30.4 %collective-permute-start.8 = (f32[4,64]{1,0:T(4,128)S(1)}, f32[4,64]{1,0:T(4,128)S(1)}, u32[]{:S(2)}, u32[]{:S(2)}) collective-permute-start(f32[4,64]{1,0:T(4,128)S(1)} %bitcast.691), channel_id=1, source_target_pairs={{0,16},{16,32},{32,48},{48,64},{64,80},{80,96},{96,112},{112,0},{1... | collective-permute-start | bytes 3080 | tf_op jit(solution)/shard_map/ppermute | solution.py:21
  154.1 30.3 %collective-permute-start.9 = (f32[4,64]{1,0:T(4,128)S(1)}, f32[4,64]{1,0:T(4,128)S(1)}, u32[]{:S(2)}, u32[]{:S(2)}) collective-permute-start(f32[4,64]{1,0:T(4,128)S(1)} %bitcast.680), channel_id=1, source_target_pairs={{16,0},{32,16},{48,32},{64,48},{80,64},{96,80},{112,96},{0,112},{1... | collective-permute-start | bytes 3080 | tf_op jit(solution)/shard_map/ppermute | solution.py:23
  218.3 13.0 %collective-permute-start.12 = (f32[4,64]{1,0:T(4,128)S(1)}, f32[4,64]{1,0:T(4,128)S(1)}, u32[]{:S(2)}, u32[]{:S(2)}) collective-permute-start(f32[4,64]{1,0:T(4,128)S(1)} %bitcast.704), channel_id=1, source_target_pairs={{0,16},{16,32},{32,48},{48,64},{64,80},{80,96},{96,112},{112,0},{1... | collective-permute-start | bytes 3080 | tf_op jit(solution)/shard_map/ppermute | solution.py:21
  218.4 12.9 %collective-permute-start.13 = (f32[4,64]{1,0:T(4,128)S(1)}, f32[4,64]{1,0:T(4,128)S(1)}, u32[]{:S(2)}, u32[]{:S(2)}) collective-permute-start(f32[4,64]{1,0:T(4,128)S(1)} %bitcast.692), channel_id=1, source_target_pairs={{16,0},{32,16},{48,32},{64,48},{80,64},{96,80},{112,96},{0,112},{1... | collective-permute-start | bytes 3080 | tf_op jit(solution)/shard_map/ppermute | solution.py:23
  222.0 9.3 %collective-permute-start.14 = (f32[4,64]{1,0:T(4,128)S(1)}, f32[4,64]{1,0:T(4,128)S(1)}, u32[]{:S(2)}, u32[]{:S(2)}) collective-permute-start(f32[4,64]{1,0:T(4,128)S(1)} %bitcast.681), channel_id=1, source_target_pairs={{0,1},{1,2},{2,3},{3,4},{4,5},{5,6},{6,7},{7,8},{8,9},{9,10},{10,1... | collective-permute-start | bytes 3080 | tf_op jit(solution)/shard_map/ppermute | solution.py:21
  236.8 9.7 %collective-permute-start.16 = (f32[4,64]{1,0:T(4,128)S(1)}, f32[4,64]{1,0:T(4,128)S(1)}, u32[]{:S(2)}, u32[]{:S(2)}) collective-permute-start(f32[4,64]{1,0:T(4,128)S(1)} %bitcast.693), channel_id=1, source_target_pairs={{0,16},{16,32},{32,48},{48,64},{64,80},{80,96},{96,112},{112,0},{1... | collective-permute-start | bytes 3080 | tf_op jit(solution)/shard_map/ppermute | solution.py:21
  236.9 9.7 %collective-permute-start.17 = (f32[4,64]{1,0:T(4,128)S(1)}, f32[4,64]{1,0:T(4,128)S(1)}, u32[]{:S(2)}, u32[]{:S(2)}) collective-permute-start(f32[4,64]{1,0:T(4,128)S(1)} %bitcast.682), channel_id=1, source_target_pairs={{16,0},{32,16},{48,32},{64,48},{80,64},{96,80},{112,96},{0,112},{1... | collective-permute-start | bytes 3080 | tf_op jit(solution)/shard_map/ppermute | solution.py:23
  253.1 8.2 %collective-permute-start.20 = (f32[4,64]{1,0:T(4,128)S(1)}, f32[4,64]{1,0:T(4,128)S(1)}, u32[]{:S(2)}, u32[]{:S(2)}) collective-permute-start(f32[4,64]{1,0:T(4,128)S(1)} %bitcast.674), channel_id=1, source_target_pairs={{0,16},{16,32},{32,48},{48,64},{64,80},{80,96},{96,112},{112,0},{1... | collective-permute-start | bytes 3080 | tf_op jit(solution)/shard_map/ppermute | solution.py:21
  253.2 8.2 %collective-permute-start.21 = (f32[4,64]{1,0:T(4,128)S(1)}, f32[4,64]{1,0:T(4,128)S(1)}, u32[]{:S(2)}, u32[]{:S(2)}) collective-permute-start(f32[4,64]{1,0:T(4,128)S(1)} %bitcast.673), channel_id=1, source_target_pairs={{16,0},{32,16},{48,32},{64,48},{80,64},{96,80},{112,96},{0,112},{1... | collective-permute-start | bytes 3080 | tf_op jit(solution)/shard_map/ppermute | solution.py:23
  486.2 8.6 %collective-permute-start.24 = (f32[4,64]{1,0:T(4,128)S(1)}, f32[4,64]{1,0:T(4,128)S(1)}, u32[]{:S(2)}, u32[]{:S(2)}) collective-permute-start(f32[4,64]{1,0:T(4,128)S(1)} %bitcast.716), channel_id=1, source_target_pairs={{0,16},{16,32},{32,48},{48,64},{64,80},{80,96},{96,112},{112,0},{1... | collective-permute-start | bytes 3080 | tf_op jit(solution)/shard_map/ppermute | solution.py:21
  486.3 8.5 %collective-permute-start.25 = (f32[4,64]{1,0:T(4,128)S(1)}, f32[4,64]{1,0:T(4,128)S(1)}, u32[]{:S(2)}, u32[]{:S(2)}) collective-permute-start(f32[4,64]{1,0:T(4,128)S(1)} %bitcast.706), channel_id=1, source_target_pairs={{16,0},{32,16},{48,32},{64,48},{80,64},{96,80},{112,96},{0,112},{1... | collective-permute-start | bytes 3080 | tf_op jit(solution)/shard_map/ppermute | solution.py:23
  502.1 8.1 %collective-permute-start.28 = (f32[4,64]{1,0:T(4,128)S(1)}, f32[4,64]{1,0:T(4,128)S(1)}, u32[]{:S(2)}, u32[]{:S(2)}) collective-permute-start(f32[4,64]{1,0:T(4,128)S(1)} %bitcast.717), channel_id=1, source_target_pairs={{0,16},{16,32},{32,48},{48,64},{64,80},{80,96},{96,112},{112,0},{1... | collective-permute-start | bytes 3080 | tf_op jit(solution)/shard_map/ppermute | solution.py:21
  534.4 8.3 %collective-permute-start.36 = (f32[4,64]{1,0:T(4,128)S(1)}, f32[4,64]{1,0:T(4,128)S(1)}, u32[]{:S(2)}, u32[]{:S(2)}) collective-permute-start(f32[4,64]{1,0:T(4,128)S(1)} %bitcast.719), channel_id=1, source_target_pairs={{0,16},{16,32},{32,48},{48,64},{64,80},{80,96},{96,112},{112,0},{1... | collective-permute-start | bytes 3080 | tf_op jit(solution)/shard_map/ppermute | solution.py:21
  534.5 8.2 %collective-permute-start.37 = (f32[4,64]{1,0:T(4,128)S(1)}, f32[4,64]{1,0:T(4,128)S(1)}, u32[]{:S(2)}, u32[]{:S(2)}) collective-permute-start(f32[4,64]{1,0:T(4,128)S(1)} %bitcast.709), channel_id=1, source_target_pairs={{16,0},{32,16},{48,32},{64,48},{80,64},{96,80},{112,96},{0,112},{1... | collective-permute-start | bytes 3080 | tf_op jit(solution)/shard_map/ppermute | solution.py:23
  610.5 8.3 %collective-permute-start.44 = (f32[4,64]{1,0:T(4,128)S(1)}, f32[4,64]{1,0:T(4,128)S(1)}, u32[]{:S(2)}, u32[]{:S(2)}) collective-permute-start(f32[4,64]{1,0:T(4,128)S(1)} %bitcast.721), channel_id=1, source_target_pairs={{0,16},{16,32},{32,48},{48,64},{64,80},{80,96},{96,112},{112,0},{1... | collective-permute-start | bytes 3080 | tf_op jit(solution)/shard_map/ppermute | solution.py:21
  610.6 8.3 %collective-permute-start.45 = (f32[4,64]{1,0:T(4,128)S(1)}, f32[4,64]{1,0:T(4,128)S(1)}, u32[]{:S(2)}, u32[]{:S(2)}) collective-permute-start(f32[4,64]{1,0:T(4,128)S(1)} %bitcast.711), channel_id=1, source_target_pairs={{16,0},{32,16},{48,32},{64,48},{80,64},{96,80},{112,96},{0,112},{1... | collective-permute-start | bytes 3080 | tf_op jit(solution)/shard_map/ppermute | solution.py:23
  (67 other events, 1012.0 us)
Sparse Core Ops, SparseCore 0:
  10.3 49.1 all-gather.1
where the time goes:
time: 707 us; the launch traced here: 694 us
  local copies, waits for them, and re-layouts  209 us (30%)
  matrix products  188 us (27%)
  starting transfers between devices  114 us (16%)
  waiting for transfers between devices  97.8 us (14%)
  blocking collectives  45.4 us (6%)
  other arithmetic  22.8 us (3%)
  between operations  16.7 us (2%)
    dot_general x81, matrix products, one_block(): return jnp.dot(parts, select, preferred_element_type=jnp.float32)  187 us
    gather x3, local copies, waits for them, and re-layouts, group_apply(): return block_product(group_values, vector[:, group_columns])  175 us
    ppermute x26, starting transfers between devices, padded(): lax.ppermute(head, axis, [((i + 1) % count, i) for i in range(ends)])  72.1 us
    ppermute x26, waiting for transfers between devices, padded(): lax.ppermute(head, axis, [((i + 1) % count, i) for i in range(ends)])  48.6 us
    all_gather x1, waiting for transfers between devices, per_device(): lax.all_gather(coarsest_values, 'span', axis=3, tiled=True)  48.5 us
    ppermute x26, starting transfers between devices, padded(): lax.ppermute(tail, axis, [(i, (i + 1) % count) for i in range(ends)])  41.5 us
    all_gather x1, blocking collectives, per_device(): group_columns = lax.all_gather(coarsest_columns, 'span', axis=1, tiled=True)  26.1 us
    all_gather x1, blocking collectives, per_device(): lax.all_gather(coarse_rhs, 'span', axis=1, tiled=True)  19.3 us
  transfers between devices with their start and end apart: 53, of which 12 were waited for; matrix products, arithmetic and copies ran while one was open for 2% of the time, Pallas kernels for 0%

commit v1 on v0

--- a/solution.py
+++ b/solution.py
@@ -176,7 +176,9 @@
         lax.all_gather(coarse_rhs, "span", axis=1, tiled=True),
         lax.all_gather(coarsest_values, "span", axis=3, tiled=True),
     )
-    group_columns = lax.all_gather(coarsest_columns, "span", axis=1, tiled=True)
+    group_columns = jnp.concatenate(
+        lax.all_to_all(jnp.stack([coarsest_columns] * lax.axis_size("span")), "span", 0, 0), axis=1
+    )
 
     def group_apply(vector):
         return block_product(group_values, vector[:, group_columns])

time: 707 us -> 692 us (0.979)
  blocking collectives: 45.4 us -> 20.1 us
  starting transfers between devices: 114 us -> 127 us
    all_gather x1 -> x0, blocking collectives: 26.1 us -> none  [per_device(): group_columns = lax.all_gather(coarsest_columns, 'span', axis=1, tiled=True)]
    all_to_all x0 -> x1, starting transfers between devices: none -> 7.63 us  [per_device(): lax.all_to_all(jnp.stack([coarsest_columns] * lax.axis_size('span')), 'sp...]
  transfers between devices with their start and end apart: 53 -> 54, of which waited for: 12 -> 11; matrix products, arithmetic and copies ran while one was open for 2% -> 16% of each run, Pallas kernels for 0% -> 0%
where the time goes in v1:
time: 692 us; the launch traced here: 682 us
  local copies, waits for them, and re-layouts  211 us (30%)
  matrix products  188 us (27%)
  starting transfers between devices  127 us (18%)
  waiting for transfers between devices  95.9 us (14%)
  other arithmetic  22.8 us (3%)
  blocking collectives  20.1 us (3%)
  between operations  16.8 us (2%)
    dot_general x81, matrix products, one_block(): return jnp.dot(parts, select, preferred_element_type=jnp.float32)  187 us
    gather x3, local copies, waits for them, and re-layouts, group_apply(): return block_product(group_values, vector[:, group_columns])  175 us
    ppermute x26, starting transfers between devices, padded(): lax.ppermute(head, axis, [((i + 1) % count, i) for i in range(ends)])  72.4 us
    all_gather x1, waiting for transfers between devices, per_device(): lax.all_gather(coarsest_values, 'span', axis=3, tiled=True)  50.7 us
    ppermute x26, starting transfers between devices, padded(): lax.ppermute(tail, axis, [(i, (i + 1) % count) for i in range(ends)])  46.4 us
    ppermute x26, waiting for transfers between devices, padded(): lax.ppermute(head, axis, [((i + 1) % count, i) for i in range(ends)])  44.4 us
    all_gather x1, blocking collectives, per_device(): lax.all_gather(coarse_rhs, 'span', axis=1, tiled=True)  20.1 us
    unnamed x87, local copies, waits for them, and re-layouts  17.4 us
  transfers between devices with their start and end apart: 54, of which 11 were waited for; matrix products, arithmetic and copies ran while one was open for 16% of the time, Pallas kernels for 0%

profile of v1, /device:TPU:1, one launch (start us, length us, event | category | flops | bytes accessed | tf_op | source)
XLA Modules:
  0.0 681.7 jit_solution(4092588035808836108)
XLA Ops:
  8.7 50.7 %all-gather.2.cloned.1.call-done = f32[8,4,4,2048]{3,2,1,0:T(4,128)} async-done(((f32[8,4,4,128]{3,2,1,0:T(4,128)}), f32[8,4,4,2048]{3,2,1,0:T(4,128)}) %all-gather.2.cloned.1.call-update) | async-done | bytes 1048592 | tf_op jit(solution)/shard_map/all_gather | solution.py:177
  72.5 7.6 %all-to-all-start = ((s32[16,8,128]{2,1,0:T(8,128)}), s32[16,8,128]{2,1,0:T(8,128)}, u32[]{:S(2)}, u32[]{:S(2)}) async-start(s32[16,8,128]{2,1,0:T(8,128)} %stack.2), calls=%async_computation | async-start | bytes 131072 | tf_op jit(solution)/shard_map/all_to_all | solution.py:180
  82.7 30.0 %while.39 = (s32[]{:T(128)}, f32[8,12,2048]{2,1,0:T(8,128)S(1)}, s32[8,2048]{1,0:T(8,128)}, bf16[12,2304]{1,0:T(8,128)(2,1)S(1)}, s32[]{:T(128)}) while((s32[]{:T(128)}, f32[8,12,2048]{2,1,0:T(8,128)S(1)}, s32[8,2048]{1,0:T(8,128)}, bf16[12,2304]{1,0:T(8,128)(2,1)S(1)}, s32[]{:T(128)}) %tuple.301), condition=%wide.region_2.0_spmd.clone, body=%wide.region_1.0_spmd.clone.sunk | while | flops 117964800 | bytes 229445 | solution.py:82
  117.5 5.6 collective-permute-start.6
  125.3 6.1 fusion.78
  131.7 23.3 %while.40 = (s32[]{:T(128)}, f32[8,12,2048]{2,1,0:T(8,128)S(1)}, s32[8,2048]{1,0:T(8,128)S(1)}, bf16[12,2304]{1,0:T(8,128)(2,1)S(1)}, s32[]{:T(128)}) while((s32[]{:T(128)}, f32[8,12,2048]{2,1,0:T(8,128)S(1)}, s32[8,2048]{1,0:T(8,128)S(1)}, bf16[12,2304]{1,0:T(8,128)(2,1)S(1)}, s32[]{:T(128)}) %tuple.347), condition=%wide.region_4.5_spmd.clone, body=%wide.region_3.0_spmd.clone.sunk | while | flops 117964800 | bytes 229445 | solution.py:82
  156.2 5.1 collective-permute-start.10
  170.5 30.5 %while.41 = (s32[]{:T(128)}, f32[8,12,2048]{2,1,0:T(8,128)S(1)}, s32[8,2048]{1,0:T(8,128)S(1)}, bf16[12,2304]{1,0:T(8,128)(2,1)}, s32[]{:T(128)}) while((s32[]{:T(128)}, f32[8,12,2048]{2,1,0:T(8,128)S(1)}, s32[8,2048]{1,0:T(8,128)S(1)}, bf16[12,2304]{1,0:T(8,128)(2,1)}, s32[]{:T(128)}) %tuple.348), condition=%wide.region_7.8_spmd.clone, body=%wide.region_6.7_spmd.clone.sunk | while | flops 117964800 | bytes 211013 | solution.py:82
  207.1 6.3 collective-permute-start.14
  247.1 5.1 collective-permute-done.23
  255.1 20.1 %all_gather.7 = f32[4,2048]{1,0:T(4,128)S(1)} all-gather(f32[4,128]{1,0:T(4,128)S(1)} %slice_add_fusion.58), channel_id=1, replica_groups=mesh['stream'=8,'span'=16] {'span'}, dimensions={1}, use_global_device_ids=true | all-gather | bytes 34816 | tf_op jit(solution)/shard_map/all_gather | solution.py:176
  276.2 54.8 %gather_fusion = f32[16384,4]{1,0:T(8,128)} fusion(f32[4,2048]{0,1:T(8,128)S(1)} %copy.181, s32[16384]{0:T(1024)S(1)} %broadcast_clamp_fusion), kind=kCustom, calls=%fused_computation | custom fusion | bytes 589824 | tf_op jit(solution)/shard_map/gather | solution.py:184
  331.0 5.3 copy.404
  339.0 60.0 %gather_fusion.1 = f32[16384,4]{1,0:T(8,128)} fusion(f32[4,2048]{0,1:T(8,128)S(1)} %copy.182, s32[16384]{0:T(1024)} %copy-done.5), kind=kCustom, calls=%fused_computation.1 | custom fusion | bytes 589824 | tf_op jit(solution)/shard_map/gather | solution.py:184
  399.1 5.2 copy.405
  406.5 60.0 %gather_fusion.2 = f32[16384,4]{1,0:T(8,128)} fusion(f32[4,2048]{0,1:T(8,128)S(1)} %copy.183, s32[16384]{0:T(1024)} %copy-done.5), kind=kCustom, calls=%fused_computation.2 | custom fusion | bytes 589824 | tf_op jit(solution)/shard_map/gather | solution.py:184
  466.5 5.3 copy.406
  477.1 5.2 collective-permute-start.26
  536.9 23.3 %while.48 = (s32[]{:T(128)}, f32[8,12,2048]{2,1,0:T(8,128)S(1)}, s32[8,2048]{1,0:T(8,128)S(1)}, bf16[12,2304]{1,0:T(8,128)(2,1)S(1)}, s32[]{:T(128)}) while((s32[]{:T(128)}, f32[8,12,2048]{2,1,0:T(8,128)S(1)}, s32[8,2048]{1,0:T(8,128)S(1)}, bf16[12,2304]{1,0:T(8,128)(2,1)S(1)}, s32[]{:T(128)}) %tuple.349), condition=%wide.region_24.25_spmd.clone, body=%wide.region_23.24_spmd.clone.sunk | while | flops 117964800 | bytes 229445 | solution.py:82
  574.1 23.3 %while.49 = (s32[]{:T(128)}, f32[8,12,2048]{2,1,0:T(8,128)S(1)}, s32[8,2048]{1,0:T(8,128)S(1)}, bf16[12,2304]{1,0:T(8,128)(2,1)S(1)}, s32[]{:T(128)}) while((s32[]{:T(128)}, f32[8,12,2048]{2,1,0:T(8,128)S(1)}, s32[8,2048]{1,0:T(8,128)S(1)}, bf16[12,2304]{1,0:T(8,128)(2,1)S(1)}, s32[]{:T(128)}) %tuple.350), condition=%wide.region_26.27_spmd.clone, body=%wide.region_25.26_spmd.clone.sunk | while | flops 117964800 | bytes 229445 | solution.py:82
  606.6 4.9 collective-permute-done.47
  611.8 23.3 %while.50 = (s32[]{:T(128)}, f32[8,12,2048]{2,1,0:T(8,128)S(1)}, s32[8,2048]{1,0:T(8,128)S(1)}, bf16[12,2304]{1,0:T(8,128)(2,1)S(1)}, s32[]{:T(128)}) while((s32[]{:T(128)}, f32[8,12,2048]{2,1,0:T(8,128)S(1)}, s32[8,2048]{1,0:T(8,128)S(1)}, bf16[12,2304]{1,0:T(8,128)(2,1)S(1)}, s32[]{:T(128)}) %tuple.351), condition=%wide.region_28.29_spmd.clone, body=%wide.region_27.28_spmd.clone.sunk | while | flops 117964800 | bytes 229445 | solution.py:82
  644.6 5.1 collective-permute-done.51
  650.0 23.3 %while.51 = (s32[]{:T(128)}, f32[8,12,2048]{2,1,0:T(8,128)S(1)}, s32[8,2048]{1,0:T(8,128)S(1)}, bf16[12,2304]{1,0:T(8,128)(2,1)S(1)}, s32[]{:T(128)}) while((s32[]{:T(128)}, f32[8,12,2048]{2,1,0:T(8,128)S(1)}, s32[8,2048]{1,0:T(8,128)S(1)}, bf16[12,2304]{1,0:T(8,128)(2,1)S(1)}, s32[]{:T(128)}) %tuple.352), condition=%wide.region_30.31_spmd.clone, body=%wide.region_29.30_spmd.clone.sunk | while | flops 117964800 | bytes 229445 | solution.py:82
  (584 shorter events, 364.8 us)
Async XLA Ops:
  7.2 52.2 %all-gather.2.cloned.1.call-start = ((), (), s32[]{:S(2)}) async-start(), calls=%async_computation.1 | async-start | bytes 1114112 | tf_op jit(solution)/shard_map/all_gather | solution.py:177
  62.6 19.7 %collective-permute-start = (f32[4,64]{1,0:T(4,128)S(1)}, f32[4,64]{1,0:T(4,128)S(1)}, u32[]{:S(2)}, u32[]{:S(2)}) collective-permute-start(f32[4,64]{1,0:T(4,128)S(1)} %bitcast.686), channel_id=1, source_target_pairs={{0,16},{16,32},{32,48},{48,64},{64,80},{80,96},{96,112},{112,0},{1... | collective-permute-start | bytes 3080 | tf_op jit(solution)/shard_map/ppermute | solution.py:21
  63.1 19.3 %collective-permute-start.1 = (f32[4,64]{1,0:T(4,128)S(1)}, f32[4,64]{1,0:T(4,128)S(1)}, u32[]{:S(2)}, u32[]{:S(2)}) collective-permute-start(f32[4,64]{1,0:T(4,128)S(1)} %bitcast.683), channel_id=1, source_target_pairs={{16,0},{32,16},{48,32},{64,48},{80,64},{96,80},{112,96},{0,112},{1... | collective-permute-start | bytes 3080 | tf_op jit(solution)/shard_map/ppermute | solution.py:23
  66.3 16.1 %collective-permute-start.2 = (f32[4,64]{1,0:T(4,128)S(1)}, f32[4,64]{1,0:T(4,128)S(1)}, u32[]{:S(2)}, u32[]{:S(2)}) collective-permute-start(f32[4,64]{1,0:T(4,128)S(1)} %bitcast.681), channel_id=1, source_target_pairs={{0,1},{1,2},{2,3},{3,4},{4,5},{5,6},{6,7},{7,8},{8,9},{9,10},{10,1... | collective-permute-start | bytes 3080 | tf_op jit(solution)/shard_map/ppermute | solution.py:21
  69.2 13.2 %collective-permute-start.3 = (f32[4,64]{1,0:T(4,128)S(1)}, f32[4,64]{1,0:T(4,128)S(1)}, u32[]{:S(2)}, u32[]{:S(2)}) collective-permute-start(f32[4,64]{1,0:T(4,128)S(1)} %bitcast.679), channel_id=1, source_target_pairs={{1,0},{2,1},{3,2},{4,3},{5,4},{6,5},{7,6},{8,7},{9,8},{10,9},{11,1... | collective-permute-start | bytes 3080 | tf_op jit(solution)/shard_map/ppermute | solution.py:23
  72.5 158.4 %all-to-all-start = ((s32[16,8,128]{2,1,0:T(8,128)}), s32[16,8,128]{2,1,0:T(8,128)}, u32[]{:S(2)}, u32[]{:S(2)}) async-start(s32[16,8,128]{2,1,0:T(8,128)} %stack.2), calls=%async_computation | async-start | bytes 131072 | tf_op jit(solution)/shard_map/all_to_all | solution.py:180
  113.9 17.5 %collective-permute-start.4 = (f32[4,64]{1,0:T(4,128)S(1)}, f32[4,64]{1,0:T(4,128)S(1)}, u32[]{:S(2)}, u32[]{:S(2)}) collective-permute-start(f32[4,64]{1,0:T(4,128)S(1)} %bitcast.718), channel_id=1, source_target_pairs={{0,16},{16,32},{32,48},{48,64},{64,80},{80,96},{96,112},{112,0},{1... | collective-permute-start | bytes 3080 | tf_op jit(solution)/shard_map/ppermute | solution.py:21
  114.0 17.4 %collective-permute-start.5 = (f32[4,64]{1,0:T(4,128)S(1)}, f32[4,64]{1,0:T(4,128)S(1)}, u32[]{:S(2)}, u32[]{:S(2)}) collective-permute-start(f32[4,64]{1,0:T(4,128)S(1)} %bitcast.709), channel_id=1, source_target_pairs={{16,0},{32,16},{48,32},{64,48},{80,64},{96,80},{112,96},{0,112},{1... | collective-permute-start | bytes 3080 | tf_op jit(solution)/shard_map/ppermute | solution.py:23
  117.5 13.9 %collective-permute-start.6 = (f32[4,64]{1,0:T(4,128)S(1)}, f32[4,64]{1,0:T(4,128)S(1)}, u32[]{:S(2)}, u32[]{:S(2)}) collective-permute-start(f32[4,64]{1,0:T(4,128)S(1)} %bitcast.699), channel_id=1, source_target_pairs={{0,1},{1,2},{2,3},{3,4},{4,5},{5,6},{6,7},{7,8},{8,9},{9,10},{10,1... | collective-permute-start | bytes 3080 | tf_op jit(solution)/shard_map/ppermute | solution.py:21
  123.1 8.3 %collective-permute-start.7 = (f32[4,64]{1,0:T(4,128)S(1)}, f32[4,64]{1,0:T(4,128)S(1)}, u32[]{:S(2)}, u32[]{:S(2)}) collective-permute-start(f32[4,64]{1,0:T(4,128)S(1)} %bitcast.689), channel_id=1, source_target_pairs={{1,0},{2,1},{3,2},{4,3},{5,4},{6,5},{7,6},{8,7},{9,8},{10,9},{11,1... | collective-permute-start | bytes 3080 | tf_op jit(solution)/shard_map/ppermute | solution.py:23
  156.2 13.3 %collective-permute-start.10 = (f32[4,64]{1,0:T(4,128)S(1)}, f32[4,64]{1,0:T(4,128)S(1)}, u32[]{:S(2)}, u32[]{:S(2)}) collective-permute-start(f32[4,64]{1,0:T(4,128)S(1)} %bitcast.692), channel_id=1, source_target_pairs={{0,1},{1,2},{2,3},{3,4},{4,5},{5,6},{6,7},{7,8},{8,9},{9,10},{10,1... | collective-permute-start | bytes 3080 | tf_op jit(solution)/shard_map/ppermute | solution.py:21
  203.4 12.8 %collective-permute-start.12 = (f32[4,64]{1,0:T(4,128)S(1)}, f32[4,64]{1,0:T(4,128)S(1)}, u32[]{:S(2)}, u32[]{:S(2)}) collective-permute-start(f32[4,64]{1,0:T(4,128)S(1)} %bitcast.680), channel_id=1, source_target_pairs={{0,16},{16,32},{32,48},{48,64},{64,80},{80,96},{96,112},{112,0},{1... | collective-permute-start | bytes 3080 | tf_op jit(solution)/shard_map/ppermute | solution.py:21
  203.5 12.7 %collective-permute-start.13 = (f32[4,64]{1,0:T(4,128)S(1)}, f32[4,64]{1,0:T(4,128)S(1)}, u32[]{:S(2)}, u32[]{:S(2)}) collective-permute-start(f32[4,64]{1,0:T(4,128)S(1)} %bitcast.678), channel_id=1, source_target_pairs={{16,0},{32,16},{48,32},{64,48},{80,64},{96,80},{112,96},{0,112},{1... | collective-permute-start | bytes 3080 | tf_op jit(solution)/shard_map/ppermute | solution.py:23
  207.1 9.1 %collective-permute-start.14 = (f32[4,64]{1,0:T(4,128)S(1)}, f32[4,64]{1,0:T(4,128)S(1)}, u32[]{:S(2)}, u32[]{:S(2)}) collective-permute-start(f32[4,64]{1,0:T(4,128)S(1)} %bitcast.677), channel_id=1, source_target_pairs={{0,1},{1,2},{2,3},{3,4},{4,5},{5,6},{6,7},{7,8},{8,9},{9,10},{10,1... | collective-permute-start | bytes 3080 | tf_op jit(solution)/shard_map/ppermute | solution.py:21
  222.8 9.0 %collective-permute-start.16 = (f32[4,64]{1,0:T(4,128)S(1)}, f32[4,64]{1,0:T(4,128)S(1)}, u32[]{:S(2)}, u32[]{:S(2)}) collective-permute-start(f32[4,64]{1,0:T(4,128)S(1)} %bitcast.700), channel_id=1, source_target_pairs={{0,16},{16,32},{32,48},{48,64},{64,80},{80,96},{96,112},{112,0},{1... | collective-permute-start | bytes 3080 | tf_op jit(solution)/shard_map/ppermute | solution.py:21
  222.8 8.9 %collective-permute-start.17 = (f32[4,64]{1,0:T(4,128)S(1)}, f32[4,64]{1,0:T(4,128)S(1)}, u32[]{:S(2)}, u32[]{:S(2)}) collective-permute-start(f32[4,64]{1,0:T(4,128)S(1)} %bitcast.690), channel_id=1, source_target_pairs={{16,0},{32,16},{48,32},{64,48},{80,64},{96,80},{112,96},{0,112},{1... | collective-permute-start | bytes 3080 | tf_op jit(solution)/shard_map/ppermute | solution.py:23
  238.8 8.3 %collective-permute-start.20 = (f32[4,64]{1,0:T(4,128)S(1)}, f32[4,64]{1,0:T(4,128)S(1)}, u32[]{:S(2)}, u32[]{:S(2)}) collective-permute-start(f32[4,64]{1,0:T(4,128)S(1)} %bitcast.720), channel_id=1, source_target_pairs={{0,16},{16,32},{32,48},{48,64},{64,80},{80,96},{96,112},{112,0},{1... | collective-permute-start | bytes 3080 | tf_op jit(solution)/shard_map/ppermute | solution.py:21
  473.4 10.7 %collective-permute-start.24 = (f32[4,64]{1,0:T(4,128)S(1)}, f32[4,64]{1,0:T(4,128)S(1)}, u32[]{:S(2)}, u32[]{:S(2)}) collective-permute-start(f32[4,64]{1,0:T(4,128)S(1)} %bitcast.721), channel_id=1, source_target_pairs={{0,16},{16,32},{32,48},{48,64},{64,80},{80,96},{96,112},{112,0},{1... | collective-permute-start | bytes 3080 | tf_op jit(solution)/shard_map/ppermute | solution.py:21
  473.5 10.7 %collective-permute-start.25 = (f32[4,64]{1,0:T(4,128)S(1)}, f32[4,64]{1,0:T(4,128)S(1)}, u32[]{:S(2)}, u32[]{:S(2)}) collective-permute-start(f32[4,64]{1,0:T(4,128)S(1)} %bitcast.712), channel_id=1, source_target_pairs={{16,0},{32,16},{48,32},{64,48},{80,64},{96,80},{112,96},{0,112},{1... | collective-permute-start | bytes 3080 | tf_op jit(solution)/shard_map/ppermute | solution.py:23
  507.2 8.3 %collective-permute-start.32 = (f32[4,64]{1,0:T(4,128)S(1)}, f32[4,64]{1,0:T(4,128)S(1)}, u32[]{:S(2)}, u32[]{:S(2)}) collective-permute-start(f32[4,64]{1,0:T(4,128)S(1)} %bitcast.723), channel_id=1, source_target_pairs={{0,16},{16,32},{32,48},{48,64},{64,80},{80,96},{96,112},{112,0},{1... | collective-permute-start | bytes 3080 | tf_op jit(solution)/shard_map/ppermute | solution.py:21
  561.2 8.3 %collective-permute-start.40 = (f32[4,64]{1,0:T(4,128)S(1)}, f32[4,64]{1,0:T(4,128)S(1)}, u32[]{:S(2)}, u32[]{:S(2)}) collective-permute-start(f32[4,64]{1,0:T(4,128)S(1)} %bitcast.725), channel_id=1, source_target_pairs={{0,16},{16,32},{32,48},{48,64},{64,80},{80,96},{96,112},{112,0},{1... | collective-permute-start | bytes 3080 | tf_op jit(solution)/shard_map/ppermute | solution.py:21
  561.3 8.3 %collective-permute-start.41 = (f32[4,64]{1,0:T(4,128)S(1)}, f32[4,64]{1,0:T(4,128)S(1)}, u32[]{:S(2)}, u32[]{:S(2)}) collective-permute-start(f32[4,64]{1,0:T(4,128)S(1)} %bitcast.716), channel_id=1, source_target_pairs={{16,0},{32,16},{48,32},{64,48},{80,64},{96,80},{112,96},{0,112},{1... | collective-permute-start | bytes 3080 | tf_op jit(solution)/shard_map/ppermute | solution.py:23
  636.2 8.4 %collective-permute-start.48 = (f32[4,64]{1,0:T(4,128)S(1)}, f32[4,64]{1,0:T(4,128)S(1)}, u32[]{:S(2)}, u32[]{:S(2)}) collective-permute-start(f32[4,64]{1,0:T(4,128)S(1)} %bitcast.727), channel_id=1, source_target_pairs={{0,16},{16,32},{32,48},{48,64},{64,80},{80,96},{96,112},{112,0},{1... | collective-permute-start | bytes 3080 | tf_op jit(solution)/shard_map/ppermute | solution.py:21
  636.3 8.3 %collective-permute-start.49 = (f32[4,64]{1,0:T(4,128)S(1)}, f32[4,64]{1,0:T(4,128)S(1)}, u32[]{:S(2)}, u32[]{:S(2)}) collective-permute-start(f32[4,64]{1,0:T(4,128)S(1)} %bitcast.719), channel_id=1, source_target_pairs={{16,0},{32,16},{48,32},{64,48},{80,64},{96,80},{112,96},{0,112},{1... | collective-permute-start | bytes 3080 | tf_op jit(solution)/shard_map/ppermute | solution.py:23
  (68 other events, 942.0 us)
Sparse Core Ops, SparseCore 0:
  10.3 49.1 all-gather.1
